TPU v7x, 512 devices: a whole 4x4x16 slice. The times are simulated.
512 devices in a mesh: seq: 32 (over z, core), mp: 16 (over y, x).
Axes of the slice: x: 4, y: 4, z: 16, core: 2. Of those that a mesh axis runs over, the one named last changes fastest.
Arguments:
- continued_prompt_entries: bfloat16 [4096, 4096], P('seq', 'mp'), may hold values from -6 to 6
- padded_prompt_entries: bfloat16 [4096, 4096], P('seq', 'mp'), may hold values from -6 to 6
- prompt_live_extents: int32 [64], P('seq'), may hold values from 8 to 64, as said below
- preceding_entry_line: bfloat16 [4096], P('mp'), may hold values from -6 to 6
- carried_memory: float32 [64, 64, 64], P('mp'), may hold values from -24 to 24
- token_mixing_ratios: float32 [5, 4096], replicated, may hold values from 0.05 to 0.95
- acceptance_transform: bfloat16 [4096, 4096], P('seq', 'mp'), may hold values from -0.09375 to 0.09375
- lookup_transform: bfloat16 [4096, 4096], P('seq', 'mp'), may hold values from -0.09375 to 0.09375
- payload_transform: bfloat16 [4096, 4096], P('seq', 'mp'), may hold values from -0.09375 to 0.09375
- gating_transform: bfloat16 [4096, 4096], P('seq', 'mp'), may hold values from -0.09375 to 0.09375
- fading_baseline: float32 [4096], P('mp'), may hold values from -10 to -3.5
- fading_left_factor: bfloat16 [4096, 128], replicated, may hold values from -0.09375 to 0.09375
- fading_right_factor: bfloat16 [128, 4096], P(None, 'mp'), may hold values from -0.5 to 0.5
- present_reward: float32 [64, 64], P('mp'), may hold values from -3 to 3
- group_layer_scaling: float32 [4096], P('mp'), may hold values from 0.5 to 1.5
- group_layer_shift_term: float32 [4096], P('mp'), may hold values from -1.8 to 1.8
- final_transform: bfloat16 [4096, 4096], P('mp', 'seq'), may hold values from -0.09375 to 0.09375
Outputs:
- mixed: bfloat16 [32, 256, 4096], P('seq', 'mp')
- span_states: float32 [32, 64, 64, 64], P('seq', 'mp')
- request_states: float32 [64, 64, 64, 64], P('seq', 'mp')
Inputs may be any that keep to these rules, and one draw needn't show every extreme that they name: `prompt_live_extents`: some request has all 64 rows live.
All inputs are finite; a program needn't handle non-finite values.
Results may differ from a plain program's by a relative error of at most 0.0076.
Values may be sent and summed in bfloat16 or wider, within the bound.
A program may use at most 64 MiB of HBM per device.

v0:
```python
import jax
import jax.numpy as jnp
from jax import lax
from jax.sharding import PartitionSpec as P

BLK = 64


norm_eps = 0.00064
highest = lax.Precision.HIGHEST


def passed_along(x, axis, by):
    length = lax.axis_size(axis)
    pairs = [(i, i + by) for i in range(length) if 0 <= i + by < length]
    return lax.ppermute(x, axis, pairs)


def entering(value, axis, join, neutral):
    count, mine = (lax.axis_size(axis), lax.axis_index(axis))
    pieces = jax.tree.map(lambda part: lax.all_gather(part, axis), value)
    total = jax.tree.map(
        lambda part, zero: jnp.full_like(part, 0) + jnp.asarray(zero, part.dtype), value, neutral
    )

    def hop(position, total):
        longer = join(total, jax.tree.map(lambda part: part[position], pieces))
        return jax.tree.map(lambda new, old: jnp.where(position < mine, new, old), longer, total)

    return lax.fori_loop(0, count - 1, hop, total)


def mix_rows(current, previous, weight):
    here = current.astype(jnp.float32)
    return (here + weight[None, :] * (previous.astype(jnp.float32) - here)).astype(jnp.bfloat16)


def block_sweep(
    evolving_memory,
    acceptance_entries,
    lookup_entries,
    payload_entries,
    log_fading_amount,
    diagonal_reward,
):
    inclusive = jnp.cumsum(log_fading_amount, axis=0)
    exclusive = inclusive - log_fading_amount
    recept_scaled = acceptance_entries * jnp.exp(exclusive)
    keys_scaled = lookup_entries * jnp.exp(-inclusive)
    scores = jnp.einsum("ihc,jhc->hij", recept_scaled, keys_scaled, precision=highest)
    count = acceptance_entries.shape[0]
    row_index = lax.broadcasted_iota(jnp.int32, (count, count), 0)
    col_index = lax.broadcasted_iota(jnp.int32, (count, count), 1)
    scores = jnp.where((row_index > col_index)[None], scores, 0.0)
    diagonal_contribution = jnp.sum(
        acceptance_entries * diagonal_reward[None] * lookup_entries, axis=-1, keepdims=True
    )
    answer_lines = (
        jnp.einsum("hij,jhd->ihd", scores, payload_entries, precision=highest)
        + diagonal_contribution * payload_entries
    )
    answer_lines = answer_lines + jnp.einsum(
        "ihc,hcd->ihd", recept_scaled, evolving_memory, precision=highest
    )
    total = inclusive[-1]
    carried = lookup_entries * jnp.exp(total[None] - inclusive)
    new_state = jnp.exp(total)[:, :, None] * evolving_memory + jnp.einsum(
        "jhc,jhd->hcd", carried, payload_entries, precision=highest
    )
    return (new_state, answer_lines)


def continued_recurrence(
    acceptance_entries, lookup_entries, payload_entries, log_fading_amount, diagonal_reward
):
    length, per_group_view, embedding_dimension = acceptance_entries.shape
    blocks = length // BLK

    def step(evolving_memory, entry_lines):
        return block_sweep(
            evolving_memory,
            entry_lines[0],
            entry_lines[1],
            entry_lines[2],
            entry_lines[3],
            diagonal_reward,
        )

    shaped = tuple(
        (
            a.reshape(blocks, BLK, per_group_view, embedding_dimension)
            for a in (acceptance_entries, lookup_entries, payload_entries, log_fading_amount)
        )
    )
    evolving_memory, results = lax.scan(
        step,
        jnp.zeros((per_group_view, embedding_dimension, embedding_dimension), jnp.float32),
        shaped,
    )
    return (evolving_memory, results.reshape(length, per_group_view, embedding_dimension))


def combine(earlier, later):
    return (earlier[0] + later[0], jnp.exp(later[0])[:, :, None] * earlier[1] + later[1])


def shifted_rows(current, edge_row, long_rows, requests, slot_rows):
    feature_part = current.shape[1]
    long_prev = jnp.concatenate([edge_row, current[: long_rows - 1]], axis=0)
    short_view = current[long_rows:].reshape(requests, slot_rows, feature_part)
    short_prev = jnp.concatenate(
        [jnp.zeros((requests, 1, feature_part), current.dtype), short_view[:, :-1]], axis=1
    )
    short_prev = short_prev.reshape(requests * slot_rows, feature_part)
    return jnp.concatenate([long_prev, short_prev], axis=0)


def on_device(
    continued_prompt_entries,
    padded_prompt_entries,
    prompt_live_extents,
    preceding_entry_line,
    carried_memory,
    token_mixing_ratios,
    acceptance_transform,
    lookup_transform,
    payload_transform,
    gating_transform,
    fading_baseline,
    fading_left_factor,
    fading_right_factor,
    present_reward,
    group_layer_scaling,
    group_layer_shift_term,
    final_transform,
):
    long_rows = continued_prompt_entries.shape[0]
    requests = prompt_live_extents.shape[0]
    slot_rows = padded_prompt_entries.shape[0] // requests
    per_group_view, embedding_dimension = present_reward.shape
    arrived = passed_along(continued_prompt_entries[-1:], "seq", 1)
    first = lax.axis_index("seq") == 0
    edge_row = jnp.where(first, preceding_entry_line[None, :], arrived)
    current = jnp.concatenate([continued_prompt_entries, padded_prompt_entries], axis=0)
    current, edge_full = (
        lax.all_gather(current, "mp", axis=1, tiled=True),
        lax.all_gather(edge_row, "mp", axis=1, tiled=True),
    )
    previous = shifted_rows(current, edge_full, long_rows, requests, slot_rows)
    mixes = [mix_rows(current, previous, token_mixing_ratios[index]) for index in range(5)]
    total_rows = current.shape[0]
    columns = acceptance_transform.shape[1]
    pieces = (
        lax.all_gather(acceptance_transform, "seq", axis=0, tiled=True),
        lax.all_gather(lookup_transform, "seq", axis=0, tiled=True),
        lax.all_gather(payload_transform, "seq", axis=0, tiled=True),
        lax.all_gather(gating_transform, "seq", axis=0, tiled=True),
    )
    acceptance_entries, lookup_entries, payload_entries, gate = tuple(
        (
            jnp.dot(source, piece, preferred_element_type=jnp.float32)
            for source, piece in zip(mixes[:4], pieces)
        )
    )
    squeezed = jnp.tanh(
        jnp.dot(mixes[4], fading_left_factor, preferred_element_type=jnp.float32)
    ).astype(jnp.bfloat16)
    log_fading_amount = -jnp.exp(
        fading_baseline[None, :]
        + jnp.dot(squeezed, fading_right_factor, preferred_element_type=jnp.float32)
    )
    recept3, keys3, values3, decay3 = [
        a.reshape(total_rows, per_group_view, embedding_dimension)
        for a in (acceptance_entries, lookup_entries, payload_entries, log_fading_amount)
    ]
    local_state, long_out = continued_recurrence(
        recept3[:long_rows],
        keys3[:long_rows],
        values3[:long_rows],
        decay3[:long_rows],
        present_reward,
    )
    long_decay = decay3[:long_rows]
    group_total = jnp.sum(long_decay, axis=0)
    blank = (
        jnp.zeros((per_group_view, embedding_dimension), jnp.float32),
        jnp.zeros((per_group_view, embedding_dimension, embedding_dimension), jnp.float32),
    )
    prefix_total, prefix_state = entering((group_total, local_state), "seq", combine, blank)
    incoming = jnp.exp(prefix_total)[:, :, None] * carried_memory + prefix_state
    before_row = jnp.cumsum(long_decay, axis=0) - long_decay
    long_out = long_out + jnp.einsum(
        "ihc,hcd->ihd", recept3[:long_rows] * jnp.exp(before_row), incoming, precision=highest
    )
    span_end = jnp.exp(group_total)[:, :, None] * incoming + local_state
    live_rows = (
        lax.broadcasted_iota(jnp.int32, (requests, slot_rows), 1) < prompt_live_extents[:, None]
    )
    live_flat = live_rows.reshape(requests * slot_rows).astype(jnp.float32)[:, None, None]
    short_shape = (requests, slot_rows, per_group_view, embedding_dimension)
    short_recept = recept3[long_rows:].reshape(short_shape)
    short_keys = (keys3[long_rows:] * live_flat).reshape(short_shape)
    short_values = values3[long_rows:].reshape(short_shape)
    short_decay = (decay3[long_rows:] * live_flat).reshape(short_shape)
    zeroed_memory = jnp.zeros(
        (per_group_view, embedding_dimension, embedding_dimension), jnp.float32
    )

    def request_pass(acceptance_lines, lookup_table, payload_table, fading_table):
        return block_sweep(
            zeroed_memory,
            acceptance_lines,
            lookup_table,
            payload_table,
            fading_table,
            present_reward,
        )

    request_states, short_out = jax.vmap(request_pass)(
        short_recept, short_keys, short_values, short_decay
    )
    wkv = jnp.concatenate(
        [long_out, short_out.reshape(requests * slot_rows, per_group_view, embedding_dimension)],
        axis=0,
    )
    mean = jnp.mean(wkv, axis=-1, keepdims=True)
    centred = wkv - mean
    variance = jnp.mean(centred * centred, axis=-1, keepdims=True)
    normed = (centred * lax.rsqrt(variance + norm_eps)).reshape(
        total_rows, columns
    ) * group_layer_scaling[None, :] + group_layer_shift_term[None, :]
    row_live = jnp.concatenate(
        [jnp.ones((long_rows,), dtype=bool), live_rows.reshape(requests * slot_rows)], axis=0
    )
    hidden = jnp.where(row_live[:, None], normed * jax.nn.silu(gate), 0.0).astype(jnp.bfloat16)
    full_out = lax.all_gather(final_transform, "seq", axis=1, tiled=True)
    mixed_rows = lax.psum_scatter(
        jnp.dot(hidden, full_out, preferred_element_type=jnp.float32),
        "mp",
        scatter_dimension=0,
        tiled=True,
    )
    return (mixed_rows.astype(jnp.bfloat16)[None], span_end[None], request_states)


def solution(mesh):
    placed = (
        P("seq", "mp"),
        P("seq", "mp"),
        P("seq"),
        P("mp"),
        P("mp", None, None),
        P(),
        P("seq", "mp"),
        P("seq", "mp"),
        P("seq", "mp"),
        P("seq", "mp"),
        P("mp"),
        P(),
        P(None, "mp"),
        P("mp", None),
        P("mp"),
        P("mp"),
        P("mp", "seq"),
    )
    return jax.shard_map(
        on_device,
        mesh=mesh,
        in_specs=placed,
        out_specs=(P("seq", "mp", None), P("seq", "mp", None, None), P("seq", "mp", None, None)),
        check_vma=False,
    )
```

profile of v0, /device:TPU:6, one launch (start us, length us, event | category | flops | bytes accessed | tf_op | source)
XLA Modules:
  0.0 631.1 jit_solution(9215683122175775181)
XLA Ops:
  7.2 1.6 pad_maximum_fusion.2
  11.7 1.7 collective-permute-start
  13.4 1.9 fusion.85
  16.0 27.2 %all_gather.34 = bf16[1,4096]{1,0:T(2,128)(2,1)} all-gather(bf16[1,256]{1,0:T(2,128)(2,1)S(1)} %broadcast_select_fusion), channel_id=1, replica_groups=mesh['seq'=32,'mp'=16] {'mp'}, dimensions={1}, use_global_device_ids=true | all-gather | bytes 8704 | tf_op jit(solution)/shard_map/all_gather | solution.py:147
  43.2 35.5 %all-gather.9.cloned.1.call-done = bf16[256,4096]{1,0:T(8,128)(2,1)} async-done(((bf16[256,256]{1,0:T(8,128)(2,1)}), bf16[256,4096]{1,0:T(8,128)(2,1)}) %all-gather.9.cloned.1.call-update) | async-done | bytes 2097168 | tf_op jit(solution)/shard_map/all_gather | solution.py:146
  78.7 1.5 slice.100
  80.1 1.2 concatenate.24
  81.4 1.1 slice.99
  82.5 3.0 fusion.41
  85.4 1.3 slice_reduce_fusion
  86.7 1.1 reshape.138
  87.8 64.6 %all-gather.15.cloned.1.call-done = bf16[4096,256]{1,0:T(8,128)(2,1)} async-done(((bf16[128,256]{1,0:T(8,128)(2,1)}), bf16[4096,256]{1,0:T(8,128)(2,1)}) %all-gather.15.cloned.1.call-update) | async-done | bytes 2097168 | tf_op jit(solution)/shard_map/all_gather | solution.py:154
  152.4 3.7 fusion.25
  157.0 66.3 %all-gather.11.cloned.1.call-done = bf16[4096,256]{1,0:T(8,128)(2,1)} async-done(((bf16[128,256]{1,0:T(8,128)(2,1)}), bf16[4096,256]{1,0:T(8,128)(2,1)}) %all-gather.11.cloned.1.call-update) | async-done | bytes 2097168 | tf_op jit(solution)/shard_map/all_gather | solution.py:155
  223.3 4.0 fusion.29
  228.1 65.8 %all-gather.13.cloned.1.call-done = bf16[4096,256]{1,0:T(8,128)(2,1)} async-done(((bf16[128,256]{1,0:T(8,128)(2,1)}), bf16[4096,256]{1,0:T(8,128)(2,1)}) %all-gather.13.cloned.1.call-update) | async-done | bytes 2097168 | tf_op jit(solution)/shard_map/all_gather | solution.py:156
  294.0 3.6 fusion.27
  298.5 13.3 %while.29 = (s32[]{:T(128)}, f32[4,64,64]{2,1,0:T(8,128)S(1)}, f32[2,64,4,64]{1,0,3,2:T(2,128)}, f32[2,64,4,64]{1,0,3,2:T(2,128)S(1)}, f32[2,64,4,64]{3,2,1,0:T(...) while((s32[]{:T(128)}, f32[4,64,64]{2,1,0:T(8,128)S(1)}, ...), condition=%wide.region_3.4_spmd.clone, body=%wide.region_0.3_spmd.clone.sunk | while | flops 51646208 | bytes 2444416 | solution.py:95
  300.4 4.3 dynamic_update_slice.6
  307.0 4.3 dynamic_update_slice.6
  314.6 32.1 %all_gather.39 = f32[32,4,64]{2,1,0:T(4,128)} all-gather(f32[1,4,64]{2,1,0:T(4,128)S(1)} %all_gather.38), channel_id=1, replica_groups=mesh['seq'=32,'mp'=16] {'seq'}, dimensions={0}, use_global_device_ids=true | all-gather | bytes 33792 | tf_op jit(solution)/shard_map/all_gather | solution.py:21
  347.5 1.2 reshape.144
  348.9 1.1 slice.94
  349.9 1.1 exponential_multiply_fusion
  351.1 1.1 reshape.143
  358.2 25.4 %all-gather.21.cloned.1.call-done = f32[128,64,64]{2,1,0:T(8,128)} async-done(((f32[4,64,64]{2,1,0:T(8,128)}), f32[128,64,64]{2,1,0:T(8,128)}) %all-gather.21.cloned.1.call-update) | async-done | bytes 2097168 | tf_op jit(solution)/shard_map/all_gather | solution.py:21
  383.7 53.9 %while.30 = (s32[]{:T(128)}, f32[4,64]{1,0:T(4,128)S(1)}, f32[4,64,64]{2,1,0:T(8,128)S(1)}, s32[]{:T(128)}, f32[32,4,64]{2,1,0:T(4,128)}, /*index=5*/f32[32,4,64,64]{3,2,1,0:T(8,128)}, s32[]{:T(128)}, s32[]{:T(128)}) while((s32[]{:T(128)}, f32[4,64]{1,0:T(4,128)S(1)}, f32[4,64,64]{2,1,0:T(8,128)S(1)}, s32[]{:T(128)}, ...), condition=%wide.region_6.7_spmd.clone, body=%wide.region_5.6_spmd.clone.sunk | while | flops 66308 | bytes 201843 | solution.py:30
  384.3 1.0 fusion.119
  396.5 1.0 fusion.119
  400.0 1.0 fusion.119
  405.2 1.0 fusion.119
  406.9 1.0 fusion.119
  408.7 1.0 fusion.119
  412.1 1.0 fusion.119
  419.0 1.0 fusion.119
  422.5 1.0 fusion.119
  433.0 1.0 fusion.119
  436.5 1.0 fusion.119
  437.6 1.8 fusion.42
  442.1 1.8 copy.102
  444.6 1.8 copy.101
  446.3 1.7 copy.99
  448.0 5.9 all-gather.17.cloned.1.call-done
  453.9 72.6 %all-gather.19.cloned.1.call-done = bf16[256,4096]{1,0:T(8,128)(2,1)} async-done(((bf16[256,128]{1,0:T(8,128)(2,1)}), bf16[256,4096]{1,0:T(8,128)(2,1)}) %all-gather.19.cloned.1.call-update) | async-done | bytes 2097168 | tf_op jit(solution)/shard_map/all_gather | solution.py:236
  526.5 7.5 %fusion.63 = f32[256,4096]{1,0:T(8,128)} fusion(bf16[256,4096]{1,0:T(8,128)(2,1)} %all-gather.19.cloned.1.call-done, f32[256,256]{1,0:T(8,128)} %copy.102, f32[256,256]{1,0:T(8,128)} %copy.101, f32[128,256]{1,0:T(8,128)} %concatenate.27, f32[128,256]{1,0:T(8,128)} %copy.99, bf16[4096,256]{1,0:T(8,128)(2,1)} %all-gather.17.cloned.1.call-done, ...), kind=kOutput, calls=%fused_computation.83 | convolution fusion | flops 1086062592 | bytes 13388032 | tf_op jit(solution)/shard_map/dot_general | solution.py:238
  534.9 1.3 convolution_add_fusion.1
  537.0 85.6 %reduce-scatter.2.cloned.1.call-done = f32[16,4096]{1,0:T(8,128)} async-done(((f32[256,4096]{1,0:T(8,128)}), f32[16,4096]{1,0:T(8,128)}) %reduce-scatter.2.cloned.1.call-update) | async-done | bytes 262160 | tf_op jit(solution)/shard_map/reduce_scatter | solution.py:237
  622.6 1.6 convert_bitcast_fusion
  (180 shorter events, 66.9 us)
Async XLA Ops:
  7.2 75.3 %copy-start = (bf16[4096,128]{1,0:T(8,128)(2,1)S(1)}, bf16[4096,128]{1,0:T(8,128)(2,1)}, u32[]{:S(2)}) copy-start(bf16[4096,128]{1,0:T(8,128)(2,1)} %param.32) | copy-start | bytes 3145732
  7.2 71.5 %all-gather.9.cloned.1.call-start = ((), (), s32[]{:S(2)}) async-start(), calls=%async_computation.1 | async-start | bytes 2228224 | tf_op jit(solution)/shard_map/all_gather | solution.py:146
  8.9 143.6 %all-gather.15.cloned.1.call-start = ((), (), s32[]{:S(2)}) async-start(), calls=%async_computation.4 | async-start | bytes 2162688 | tf_op jit(solution)/shard_map/all_gather | solution.py:154
  9.6 213.7 %all-gather.11.cloned.1.call-start = ((), (), s32[]{:S(2)}) async-start(), calls=%async_computation.2 | async-start | bytes 2162688 | tf_op jit(solution)/shard_map/all_gather | solution.py:155
  10.4 283.6 %all-gather.13.cloned.1.call-start = ((), (), s32[]{:S(2)}) async-start(), calls=%async_computation.3 | async-start | bytes 2162688 | tf_op jit(solution)/shard_map/all_gather | solution.py:156
  10.9 372.7 %all-gather.21.cloned.1.call-start = ((), (), s32[]{:S(2)}) async-start(), calls=%async_computation.8 | async-start | bytes 4325376 | tf_op jit(solution)/shard_map/all_gather | solution.py:21
  11.7 3.7 collective-permute-start
  78.7 2.7 copy-start.3
  223.3 70.7 %copy-start.8 = (bf16[2,64,4096]{2,1,0:T(8,128)(2,1)S(1)}, bf16[2,64,4096]{2,1,0:T(8,128)(2,1)}, u32[]{:S(2)}) copy-start(bf16[2,64,4096]{2,1,0:T(8,128)(2,1)} %concatenate.24) | copy-start | bytes 3145732
  223.3 70.7 %copy-start.14 = (bf16[1,4096]{1,0:T(2,128)(2,1)S(1)}, bf16[1,4096]{1,0:T(2,128)(2,1)}, u32[]{:S(2)}) copy-start(bf16[1,4096]{1,0:T(2,128)(2,1)} %all_gather.34) | copy-start | bytes 24580
  294.0 4.5 copy-start.13
  298.4 15.4 %copy-start.16 = (s32[2]{0:T(128)S(1)}, s32[2]{0:T(128)}, u32[]{:S(2)}) copy-start(s32[2]{0:T(128)} %param.23) | copy-start | bytes 28
  298.4 16.1 %copy-start.15 = (f32[256]{0:T(256)S(1)}, f32[256]{0:T(256)}, u32[]{:S(2)}) copy-start(f32[256]{0:T(256)} %get-tuple-element.272) | copy-start | bytes 3076
  298.5 48.3 %copy-start.6 = (f32[128,256]{0,1:T(8,128)S(1)}, f32[128,256]{0,1:T(8,128)}, u32[]{:S(2)}) copy-start(f32[128,256]{0,1:T(8,128)} %get-tuple-element.274) | copy-start | bytes 393220
  298.5 48.4 %copy-start.10 = (f32[128,256]{0,1:T(8,128)S(1)}, f32[128,256]{0,1:T(8,128)}, u32[]{:S(2)}) copy-start(f32[128,256]{0,1:T(8,128)} %get-tuple-element.273) | copy-start | bytes 393220
  311.7 0.7 copy-start.1
  312.4 141.5 %all-gather.17.cloned.1.call-start = ((), (), s32[]{:S(2)}) async-start(), calls=%async_computation.5 | async-start | bytes 2162688 | tf_op jit(solution)/shard_map/all_gather | solution.py:157
  313.0 213.5 %all-gather.19.cloned.1.call-start = ((), (), s32[]{:S(2)}) async-start(), calls=%async_computation.6 | async-start | bytes 2162688 | tf_op jit(solution)/shard_map/all_gather | solution.py:236
  313.7 308.9 %reduce-scatter.2.cloned.1.call-start = ((), (), s32[]{:S(2)}) async-start(), calls=%async_computation.7 | async-start | bytes 4456448 | tf_op jit(solution)/shard_map/reduce_scatter | solution.py:237
  347.3 7.4 %copy-start.12 = (f32[2,64,4,64]{1,0,3,2:T(2,128)S(1)}, f32[2,64,4,64]{1,0,3,2:T(2,128)}, u32[]{:S(2)}) copy-start(f32[2,64,4,64]{1,0,3,2:T(2,128)} %get-tuple-element.156) | copy-start | bytes 393220
  347.5 5.4 copy-start.7
  354.5 171.9 %copy-start.17 = (f32[256]{0:T(256)S(1)}, f32[256]{0:T(256)}, u32[]{:S(2)}) copy-start(f32[256]{0:T(256)} %param.36) | copy-start | bytes 3076
  358.2 168.2 %copy-start.4 = (bf16[256,4096]{1,0:T(8,128)(2,1)S(1)}, bf16[256,4096]{1,0:T(8,128)(2,1)}, u32[]{:S(2)}) copy-start(bf16[256,4096]{1,0:T(8,128)(2,1)} %all-gather.9.cloned.1.call-done) | copy-start | bytes 6291460
  439.4 1.0 copy-start.5
  534.0 0.9 copy-start.9
  534.0 2.3 copy-start.2
  534.0 2.3 copy-start.11
Sparse Core Ops, SparseCore 0:
  11.6 67.0 all-gather.8
  80.8 71.5 all-gather.14
  154.5 68.6 all-gather.10
  225.2 68.6 all-gather.12
  312.5 71.0 all-gather.20
  385.6 68.2 all-gather.16
  456.0 70.4 all-gather.18
  534.1 88.4 reduce-scatter.1
where the time goes:
time: 633 us; the launch traced here: 631 us
  waiting for transfers between devices  425 us (67%)
  other arithmetic  64.5 us (10%)
  blocking collectives  59.4 us (9%)
  local copies, waits for them, and re-layouts  35.3 us (6%)
  matrix products  29.4 us (5%)
  between operations  14.5 us (2%)
    reduce_scatter x1, waiting for transfers between devices, on_device(): lax.psum_scatter(jnp.dot(hidden, full_out, preferred_element_type=jnp.flo...  85.6 us
    all_gather x1, waiting for transfers between devices, on_device(): full_out = lax.all_gather(final_transform, 'seq', axis=1, tiled=True)  72.6 us
    all_gather x1, waiting for transfers between devices, on_device(): lax.all_gather(lookup_transform, 'seq', axis=0, tiled=True)  66.3 us
    all_gather x1, waiting for transfers between devices, on_device(): lax.all_gather(payload_transform, 'seq', axis=0, tiled=True)  65.8 us
    all_gather x1, waiting for transfers between devices, on_device(): lax.all_gather(acceptance_transform, 'seq', axis=0, tiled=True)  64.6 us
    all_gather x1, waiting for transfers between devices, on_device(): lax.all_gather(current, 'mp', axis=1, tiled=True)  35.5 us
    all_gather x1, blocking collectives, entering(): pieces = jax.tree.map(lambda part: lax.all_gather(part, axis), value)  32.1 us
    select_n x31, other arithmetic, hop(): jnp.where(position < mine, new, old)  32 us
  transfers between devices with their start and end apart: 9, of which 8 were waited for; matrix products, arithmetic and copies ran while one was open for 16% of the time, Pallas kernels for 0%

commit v1 on v0

--- a/solution.py
+++ b/solution.py
@@ -4,30 +4,33 @@
 from jax.sharding import PartitionSpec as P
 
 BLK = 64
+SEQ = ("z", "core")
 
 
 norm_eps = 0.00064
 highest = lax.Precision.HIGHEST
 
 
-def passed_along(x, axis, by):
-    length = lax.axis_size(axis)
-    pairs = [(i, i + by) for i in range(length) if 0 <= i + by < length]
-    return lax.ppermute(x, axis, pairs)
-
-
-def entering(value, axis, join, neutral):
-    count, mine = (lax.axis_size(axis), lax.axis_index(axis))
-    pieces = jax.tree.map(lambda part: lax.all_gather(part, axis), value)
-    total = jax.tree.map(
-        lambda part, zero: jnp.full_like(part, 0) + jnp.asarray(zero, part.dtype), value, neutral
-    )
-
-    def hop(position, total):
-        longer = join(total, jax.tree.map(lambda part: part[position], pieces))
-        return jax.tree.map(lambda new, old: jnp.where(position < mine, new, old), longer, total)
-
-    return lax.fori_loop(0, count - 1, hop, total)
+def seq_index():
+    return lax.axis_index("z") * lax.axis_size("core") + lax.axis_index("core")
+
+
+def seq_shift(x, by, length):
+    pairs = [(i, i + by) for i in range(length) if i + by < length]
+    return lax.ppermute(x, SEQ, pairs)
+
+
+def exclusive_prefix(value, start, length):
+    mine = seq_index()
+    arrived = seq_shift(value, 1, length)
+    total = jax.tree.map(lambda got, first: jnp.where(mine == 0, first, got), arrived, start)
+    step = 1
+    while step < length:
+        got = seq_shift(total, step, length)
+        joined = combine(got, total)
+        total = jax.tree.map(lambda new, old: jnp.where(mine >= step, new, old), joined, total)
+        step *= 2
+    return total
 
 
 def mix_rows(current, previous, weight):
@@ -138,24 +141,26 @@
     requests = prompt_live_extents.shape[0]
     slot_rows = padded_prompt_entries.shape[0] // requests
     per_group_view, embedding_dimension = present_reward.shape
-    arrived = passed_along(continued_prompt_entries[-1:], "seq", 1)
-    first = lax.axis_index("seq") == 0
+    seq_count = lax.axis_size("z") * lax.axis_size("core")
+    arrived = seq_shift(continued_prompt_entries[-1:], 1, seq_count)
+    first = seq_index() == 0
     edge_row = jnp.where(first, preceding_entry_line[None, :], arrived)
-    current = jnp.concatenate([continued_prompt_entries, padded_prompt_entries], axis=0)
-    current, edge_full = (
-        lax.all_gather(current, "mp", axis=1, tiled=True),
-        lax.all_gather(edge_row, "mp", axis=1, tiled=True),
-    )
+    stacked = jnp.concatenate([continued_prompt_entries, padded_prompt_entries, edge_row], axis=0)
+    stacked = lax.all_gather(stacked, "mp", axis=1, tiled=True)
+    current = stacked[: long_rows + padded_prompt_entries.shape[0]]
+    edge_full = stacked[-1:]
     previous = shifted_rows(current, edge_full, long_rows, requests, slot_rows)
     mixes = [mix_rows(current, previous, token_mixing_ratios[index]) for index in range(5)]
     total_rows = current.shape[0]
     columns = acceptance_transform.shape[1]
-    pieces = (
-        lax.all_gather(acceptance_transform, "seq", axis=0, tiled=True),
-        lax.all_gather(lookup_transform, "seq", axis=0, tiled=True),
-        lax.all_gather(payload_transform, "seq", axis=0, tiled=True),
-        lax.all_gather(gating_transform, "seq", axis=0, tiled=True),
-    )
+    blocks = jnp.stack(
+        [acceptance_transform, lookup_transform, payload_transform, gating_transform, final_transform.T],
+        axis=0,
+    )
+    blocks = lax.all_gather(lax.all_gather(blocks, "z"), "core")
+    cores, chips, kinds, depth, width = blocks.shape
+    blocks = jnp.transpose(blocks, (2, 1, 0, 3, 4)).reshape(kinds, chips * cores * depth, width)
+    pieces = tuple(blocks[index] for index in range(4))
     acceptance_entries, lookup_entries, payload_entries, gate = tuple(
         (
             jnp.dot(source, piece, preferred_element_type=jnp.float32)
@@ -182,12 +187,8 @@
     )
     long_decay = decay3[:long_rows]
     group_total = jnp.sum(long_decay, axis=0)
-    blank = (
-        jnp.zeros((per_group_view, embedding_dimension), jnp.float32),
-        jnp.zeros((per_group_view, embedding_dimension, embedding_dimension), jnp.float32),
-    )
-    prefix_total, prefix_state = entering((group_total, local_state), "seq", combine, blank)
-    incoming = jnp.exp(prefix_total)[:, :, None] * carried_memory + prefix_state
+    start = (jnp.zeros((per_group_view, embedding_dimension), jnp.float32), carried_memory)
+    _, incoming = exclusive_prefix((group_total, local_state), start, seq_count)
     before_row = jnp.cumsum(long_decay, axis=0) - long_decay
     long_out = long_out + jnp.einsum(
         "ihc,hcd->ihd", recept3[:long_rows] * jnp.exp(before_row), incoming, precision=highest
@@ -233,9 +234,11 @@
         [jnp.ones((long_rows,), dtype=bool), live_rows.reshape(requests * slot_rows)], axis=0
     )
     hidden = jnp.where(row_live[:, None], normed * jax.nn.silu(gate), 0.0).astype(jnp.bfloat16)
-    full_out = lax.all_gather(final_transform, "seq", axis=1, tiled=True)
+    full_out = blocks[4]
     mixed_rows = lax.psum_scatter(
-        jnp.dot(hidden, full_out, preferred_element_type=jnp.float32),
+        lax.dot_general(
+            hidden, full_out, (((1,), (1,)), ((), ())), preferred_element_type=jnp.float32
+        ),
         "mp",
         scatter_dimension=0,
         tiled=True,
@@ -262,11 +265,17 @@
         P("mp"),
         P("mp"),
         P("mp", "seq"),
+    )
+    devices = mesh.devices
+    seq_devices, mp_devices = devices.shape
+    mesh = jax.sharding.Mesh(devices.reshape(seq_devices // 2, 2, mp_devices), ("z", "core", "mp"))
+    placed = tuple(
+        P(*[SEQ if name == "seq" else name for name in spec]) for spec in placed
     )
     return jax.shard_map(
         on_device,
         mesh=mesh,
         in_specs=placed,
-        out_specs=(P("seq", "mp", None), P("seq", "mp", None, None), P("seq", "mp", None, None)),
+        out_specs=(P(SEQ, "mp", None), P(SEQ, "mp", None, None), P(SEQ, "mp", None, None)),
         check_vma=False,
     )

time: 633 us -> 409 us (0.65)
  the two profiles are of different devices: /device:TPU:6 before, /device:TPU:2 now
where the time goes in v1:
time: 409 us; the launch traced here: 407 us
  waiting for transfers between devices  232 us (57%)
  starting transfers between devices  72.5 us (18%)
  local copies, waits for them, and re-layouts  54.7 us (13%)
  matrix products  21.7 us (5%)
  between operations  14.5 us (4%)
  other arithmetic  11.6 us (3%)
    all_gather x2, waiting for transfers between devices, on_device(): blocks = lax.all_gather(lax.all_gather(blocks, 'z'), 'core')  80.3 us
    reduce_scatter x1, waiting for transfers between devices, on_device(): lax.psum_scatter(lax.dot_general(hidden, full_out, (((1,), (1,)), ((), ()...  80.1 us
    ppermute x12, starting transfers between devices, seq_shift(): return lax.ppermute(x, SEQ, pairs)  72.3 us
    all_gather x1, waiting for transfers between devices, on_device(): stacked = lax.all_gather(stacked, 'mp', axis=1, tiled=True)  60.9 us
    ppermute x12, waiting for transfers between devices, seq_shift(): return lax.ppermute(x, SEQ, pairs)  10.7 us
    unnamed x71, local copies, waits for them, and re-layouts  10.1 us
    dynamic_update_slice x4, local copies, waits for them, and re-layouts, continued_recurrence(): lax.scan(step, jnp.zeros((per_group_view, embedding_dimension, embedding_...  8.76 us
  transfers between devices with their start and end apart: 16, of which 10 were waited for; matrix products, arithmetic and copies ran while one was open for 14% of the time, Pallas kernels for 0%

profile of v1, /device:TPU:2, one launch (start us, length us, event | category | flops | bytes accessed | tf_op | source)
XLA Modules:
  0.0 407.3 jit_solution(4726152788664702614)
XLA Ops:
  8.1 0.9 copy.128
  13.1 1.7 collective-permute-start
  16.3 1.5 pad_maximum_fusion.2
  17.9 80.3 %all-gather.8.cloned.1.call-done = bf16[80,128,256]{2,1,0:T(8,128)(2,1)} async-done(((bf16[5,128,256]{2,1,0:T(8,128)(2,1)}), bf16[80,128,256]{2,1,0:T(8,128)(2,1)}) %all-gather.8.cloned.1.call-update) | async-done | bytes 5242896 | tf_op jit(solution)/shard_map/all_gather | solution.py:160
  99.8 60.9 %all-gather.6.cloned.1.call-done = bf16[257,4096]{1,0:T(8,128)(2,1)} async-done(((bf16[257,256]{1,0:T(8,128)(2,1)}), bf16[257,4096]{1,0:T(8,128)(2,1)}) %all-gather.6.cloned.1.call-update) | async-done | bytes 2105360 | tf_op jit(solution)/shard_map/all_gather | solution.py:149
  160.7 1.9 slice-done
  163.0 1.0 copy-done.15
  164.0 3.0 fusion.40
  167.2 1.3 collective-permute-start.1
  169.3 4.1 %collective-permute-start.2 = (f32[4,64]{1,0:T(4,128)S(1)}, f32[4,64]{1,0:T(4,128)S(1)}, u32[]{:S(2)}, u32[]{:S(2)}) collective-permute-start(f32[4,64]{1,0:T(4,128)S(1)} %get-tuple-element.130), channel_id=1, source_target_pairs={{0,16},{16,32},{32,48},{48,64},{64,80},{80,96},{96,112},{112,128},... | collective-permute-start | bytes 3080 | tf_op jit(solution)/shard_map/ppermute | solution.py:20
  174.4 6.0 %collective-permute-start.3 = (f32[4,64]{1,0:T(4,128)S(1)}, f32[4,64]{1,0:T(4,128)S(1)}, u32[]{:S(2)}, u32[]{:S(2)}) collective-permute-start(f32[4,64]{1,0:T(4,128)S(1)} %get-tuple-element.128), channel_id=1, source_target_pairs={{0,32},{16,48},{32,64},{48,80},{64,96},{80,112},{96,128},{112,144}... | collective-permute-start | bytes 3080 | tf_op jit(solution)/shard_map/ppermute | solution.py:20
  180.7 1.1 collective-permute-done.3
  181.8 5.2 %collective-permute-start.4 = (f32[4,64]{1,0:T(4,128)S(1)}, f32[4,64]{1,0:T(4,128)S(1)}, u32[]{:S(2)}, u32[]{:S(2)}) collective-permute-start(f32[4,64]{1,0:T(4,128)S(1)} %get-tuple-element.126), channel_id=1, source_target_pairs={{0,64},{16,80},{32,96},{48,112},{64,128},{80,144},{96,160},{112,17... | collective-permute-start | bytes 3080 | tf_op jit(solution)/shard_map/ppermute | solution.py:20
  188.2 13.1 %collective-permute-start.5 = (f32[4,64]{1,0:T(4,128)S(1)}, f32[4,64]{1,0:T(4,128)S(1)}, u32[]{:S(2)}, u32[]{:S(2)}) collective-permute-start(f32[4,64]{1,0:T(4,128)S(1)} %get-tuple-element.124), channel_id=1, source_target_pairs={{0,128},{16,144},{32,160},{48,176},{64,192},{80,208},{96,224},{112... | collective-permute-start | bytes 3080 | tf_op jit(solution)/shard_map/ppermute | solution.py:20
  201.4 6.2 %fusion.92 = (bf16[1,16,2,128,256]{4,3,0,1,2:T(8,128)(2,1)}, bf16[1,16,2,128,256]{4,3,0,1,2:T(8,128)(2,1)}, bf16[1,16,2,128,256]{4,3,0,1,2:T(8,128)(2,1)S(1)}, b...) fusion(bf16[5,16,2,128,256]{4,3,0,1,2:T(8,128)(2,1)} %bitcast.142), kind=kLoop, calls=%fused_computation.139 | loop fusion | bytes 20971520 | tf_op jit(solution)/shard_map/slice | solution.py:163
  207.8 1.4 copy-done.3
  209.5 1.1 fusion.26
  212.0 1.1 fusion.28
  214.4 1.5 fusion.24
  217.1 13.2 %while.13 = (s32[]{:T(128)}, f32[4,64,64]{2,1,0:T(8,128)S(1)}, f32[2,64,4,64]{1,0,3,2:T(2,128)}, f32[2,64,4,64]{1,0,3,2:T(2,128)S(1)}, f32[2,64,4,64]{3,2,1,0:T(...) while((s32[]{:T(128)}, f32[4,64,64]{2,1,0:T(8,128)S(1)}, ...), condition=%wide.region_3.4_spmd.clone, body=%wide.region_0.3_spmd.clone.sunk | while | flops 51646208 | bytes 2444424 | solution.py:98
  219.4 4.3 %dynamic_update_slice.6 = f32[2,64,4,64]{1,0,3,2:T(2,128)} dynamic-update-slice(f32[2,64,4,64]{1,0,3,2:T(2,128)} %get-tuple-element.235, f32[1,64,4,64]{1,0,3,2:T(1,128)S(1)} %copy.218, s32[]{:T(128)S(6)} %copy.227, s32[]{:T(128)} %constant.28.clone.1..sunk, s32[]{:T(128)} %constant.28.clone.1..sunk, s32[]{:T(128)} %constant.28.clone.1..sunk) | dynamic-update-slice | bytes 131076 | tf_op jit(solution)/shard_map/while/body/jit(dynamic_update_index_in_dim)/dynamic_update_slice | solution.py:98
  226.1 4.3 %dynamic_update_slice.6 = f32[2,64,4,64]{1,0,3,2:T(2,128)} dynamic-update-slice(f32[2,64,4,64]{1,0,3,2:T(2,128)} %get-tuple-element.235, f32[1,64,4,64]{1,0,3,2:T(1,128)S(1)} %copy.218, s32[]{:T(128)S(6)} %copy.227, s32[]{:T(128)} %constant.28.clone.1..sunk, s32[]{:T(128)} %constant.28.clone.1..sunk, s32[]{:T(128)} %constant.28.clone.1..sunk) | dynamic-update-slice | bytes 131076 | tf_op jit(solution)/shard_map/while/body/jit(dynamic_update_index_in_dim)/dynamic_update_slice | solution.py:98
  230.3 1.3 collective-permute-start.6
  231.7 1.1 slice.127
  232.7 1.1 reshape.150
  234.0 0.9 broadcast_select_fusion
  235.0 1.5 collective-permute-start.7
  236.5 2.1 exponential_multiply_fusion
  238.6 5.3 %collective-permute-start.8 = (f32[4,64,64]{2,1,0:T(8,128)S(1)}, f32[4,64,64]{2,1,0:T(8,128)S(1)}, u32[]{:S(2)}, u32[]{:S(2)}) collective-permute-start(f32[4,64,64]{2,1,0:T(8,128)S(1)} %add_select_fusion.4), channel_id=1, source_target_pairs={{0,32},{16,48},{32,64},{48,80},{64,96},{80,112},{96,128},{112,144}... | collective-permute-start | bytes 196616 | tf_op jit(solution)/shard_map/ppermute | solution.py:20
  244.9 2.5 collective-permute-done.8
  247.5 6.3 %collective-permute-start.9 = (f32[4,64,64]{2,1,0:T(8,128)S(1)}, f32[4,64,64]{2,1,0:T(8,128)S(1)}, u32[]{:S(2)}, u32[]{:S(2)}) collective-permute-start(f32[4,64,64]{2,1,0:T(8,128)S(1)} %add_select_fusion.3), channel_id=1, source_target_pairs={{0,64},{16,80},{32,96},{48,112},{64,128},{80,144},{96,160},{112,17... | collective-permute-start | bytes 196616 | tf_op jit(solution)/shard_map/ppermute | solution.py:20
  254.4 3.2 collective-permute-done.9
  257.7 12.6 %collective-permute-start.10 = (f32[4,64,64]{2,1,0:T(8,128)S(1)}, f32[4,64,64]{2,1,0:T(8,128)S(1)}, u32[]{:S(2)}, u32[]{:S(2)}) collective-permute-start(f32[4,64,64]{2,1,0:T(8,128)S(1)} %add_select_fusion.2), channel_id=1, source_target_pairs={{0,128},{16,144},{32,160},{48,176},{64,192},{80,208},{96,224},{112... | collective-permute-start | bytes 196616 | tf_op jit(solution)/shard_map/ppermute | solution.py:20
  271.4 1.5 collective-permute-done.10
  273.0 13.9 %collective-permute-start.11 = (f32[4,64,64]{2,1,0:T(8,128)S(1)}, f32[4,64,64]{2,1,0:T(8,128)}, u32[]{:S(2)}, u32[]{:S(2)}) collective-permute-start(f32[4,64,64]{2,1,0:T(8,128)S(1)} %add_select_fusion.1), channel_id=1, source_target_pairs={{0,256},{16,272},{32,288},{48,304},{64,320},{80,336},{96,352},{112... | collective-permute-start | bytes 196616 | tf_op jit(solution)/shard_map/ppermute | solution.py:20
  289.5 3.3 copy.156
  292.8 1.8 reshape.151
  294.6 1.8 reshape.148
  296.4 1.8 concatenate.27
  298.2 1.5 copy.155
  299.8 1.8 fusion.41
  302.4 1.8 copy.154
  304.9 1.8 copy.153
  307.5 7.5 %fusion.68 = f32[256,4096]{1,0:T(8,128)} fusion(bf16[4096,256]{1,0:T(8,128)(2,1)} %bitcast.145, f32[256,256]{1,0:T(8,128)} %copy.154, f32[256,256]{1,0:T(8,128)} %copy.153, f32[128,256]{1,0:T(8,128)} %concatenate.27, f32[128,256]{1,0:T(8,128)} %copy.151, bf16[4096,256]{1,0:T(8,128)(2,1)} %bitcast.146, f32[4096]{0:T(1024)S(1)} %bitcast.160, ...), kind=kOutput, calls=%fused_computation.84 | convolution fusion | flops 1086062592 | bytes 13396480 | tf_op jit(solution)/shard_map/dot_general | solution.py:239
  316.0 1.3 convolution_add_fusion.1
  317.3 1.7 add_bitcast_fusion
  319.0 80.1 %reduce-scatter.2.cloned.1.call-done = f32[16,4096]{1,0:T(8,128)} async-done(((f32[256,4096]{1,0:T(8,128)}), f32[16,4096]{1,0:T(8,128)}) %reduce-scatter.2.cloned.1.call-update) | async-done | bytes 262160 | tf_op jit(solution)/shard_map/reduce_scatter | solution.py:238
  399.1 1.6 convert_bitcast_fusion
  (175 shorter events, 29.7 us)
Async XLA Ops:
  7.2 156.8 %copy-start = (bf16[4096,128]{1,0:T(8,128)(2,1)S(1)}, bf16[4096,128]{1,0:T(8,128)(2,1)}, u32[]{:S(2)}) copy-start(bf16[4096,128]{1,0:T(8,128)(2,1)} %param.30) | copy-start | bytes 3145732
  7.2 91.1 %all-gather.8.cloned.1.call-start = ((), (), s32[]{:S(2)}) async-start(), calls=%async_computation.3 | async-start | bytes 5570560 | tf_op jit(solution)/shard_map/all_gather | solution.py:160
  12.4 148.3 %all-gather.6.cloned.1.call-start = ((), (), s32[]{:S(2)}) async-start(), calls=%async_computation.1 | async-start | bytes 2297856 | tf_op jit(solution)/shard_map/all_gather | solution.py:149
  13.1 2.5 collective-permute-start
  17.9 183.5 %all-gather.10.cloned.1.call-start = ((), (), s32[]{:S(2)}) async-start(), calls=%async_computation.4 | async-start | bytes 15728640 | tf_op jit(solution)/shard_map/all_gather | solution.py:160
  98.2 0.9 copy-start.23
  98.3 300.9 %reduce-scatter.2.cloned.1.call-start = ((), (), s32[]{:S(2)}) async-start(), calls=%async_computation.2 | async-start | bytes 4456448 | tf_op jit(solution)/shard_map/reduce_scatter | solution.py:238
  160.7 1.9 slice-start
  160.7 2.1 copy-start.2
  162.9 4.1 %copy-start.13 = (bf16[2,64,4096]{2,1,0:T(8,128)(2,1)}, bf16[2,64,4096]{2,1,0:T(8,128)(2,1)S(1)}, u32[]{:S(2)}) copy-start(bf16[2,64,4096]{2,1,0:T(8,128)(2,1)S(1)} %concatenate.24) | copy-start | bytes 3145732
  162.9 1.0 copy-start.15
  163.0 4.0 copy-start.27
  164.0 4.5 %copy-start.29 = (s32[2]{0:T(128)S(1)}, s32[2]{0:T(128)}, u32[]{:S(2)}) copy-start(s32[2]{0:T(128)} %param.21) | copy-start | bytes 28
  167.2 2.1 collective-permute-start.1
  169.3 5.1 %collective-permute-start.2 = (f32[4,64]{1,0:T(4,128)S(1)}, f32[4,64]{1,0:T(4,128)S(1)}, u32[]{:S(2)}, u32[]{:S(2)}) collective-permute-start(f32[4,64]{1,0:T(4,128)S(1)} %get-tuple-element.130), channel_id=1, source_target_pairs={{0,16},{16,32},{32,48},{48,64},{64,80},{80,96},{96,112},{112,128},... | collective-permute-start | bytes 3080 | tf_op jit(solution)/shard_map/ppermute | solution.py:20
  174.4 33.2 %copy-start.7 = (f32[2,64,4,64]{3,2,1,0:T(4,128)}, f32[2,64,4,64]{3,2,1,0:T(4,128)S(1)}, u32[]{:S(2)}) copy-start(f32[2,64,4,64]{3,2,1,0:T(4,128)S(1)} %copy.141) | copy-start | bytes 393220
  174.4 7.3 %collective-permute-start.3 = (f32[4,64]{1,0:T(4,128)S(1)}, f32[4,64]{1,0:T(4,128)S(1)}, u32[]{:S(2)}, u32[]{:S(2)}) collective-permute-start(f32[4,64]{1,0:T(4,128)S(1)} %get-tuple-element.128), channel_id=1, source_target_pairs={{0,32},{16,48},{32,64},{48,80},{64,96},{80,112},{96,128},{112,144}... | collective-permute-start | bytes 3080 | tf_op jit(solution)/shard_map/ppermute | solution.py:20
  180.7 6.3 %copy-start.12 = (f32[2,64,4,64]{3,2,1,0:T(4,128)}, f32[2,64,4,64]{3,2,1,0:T(4,128)S(1)}, u32[]{:S(2)}) copy-start(f32[2,64,4,64]{3,2,1,0:T(4,128)S(1)} %fusion.72) | copy-start | bytes 393220
  181.8 6.5 %collective-permute-start.4 = (f32[4,64]{1,0:T(4,128)S(1)}, f32[4,64]{1,0:T(4,128)S(1)}, u32[]{:S(2)}, u32[]{:S(2)}) collective-permute-start(f32[4,64]{1,0:T(4,128)S(1)} %get-tuple-element.126), channel_id=1, source_target_pairs={{0,64},{16,80},{32,96},{48,112},{64,128},{80,144},{96,160},{112,17... | collective-permute-start | bytes 3080 | tf_op jit(solution)/shard_map/ppermute | solution.py:20
  188.2 43.4 %collective-permute-start.5 = (f32[4,64]{1,0:T(4,128)S(1)}, f32[4,64]{1,0:T(4,128)S(1)}, u32[]{:S(2)}, u32[]{:S(2)}) collective-permute-start(f32[4,64]{1,0:T(4,128)S(1)} %get-tuple-element.124), channel_id=1, source_target_pairs={{0,128},{16,144},{32,160},{48,176},{64,192},{80,208},{96,224},{112... | collective-permute-start | bytes 3080 | tf_op jit(solution)/shard_map/ppermute | solution.py:20
  201.4 6.4 %copy-start.16 = (bf16[127,4096]{1,0:T(8,128)(2,1)S(1)}, bf16[127,4096]{1,0:T(8,128)(2,1)}, u32[]{:S(2)}) copy-start(bf16[127,4096]{1,0:T(8,128)(2,1)} %copy-done.15) | copy-start | bytes 3121156
  207.6 1.6 copy-start.3
  207.6 1.9 copy-start.14
  207.6 1.9 copy-start.26
  207.6 1.9 copy-start.28
  211.2 0.7 copy-start.25
  214.4 2.7 copy-start.22
  230.3 3.7 collective-permute-start.6
  232.7 11.8 %copy-start.19 = (f32[128,256]{1,0:T(8,128)S(1)}, f32[128,256]{1,0:T(8,128)}, u32[]{:S(2)}) copy-start(f32[128,256]{1,0:T(8,128)} %get-tuple-element.152) | copy-start | bytes 393220
  235.0 3.5 collective-permute-start.7
  238.6 8.7 %collective-permute-start.8 = (f32[4,64,64]{2,1,0:T(8,128)S(1)}, f32[4,64,64]{2,1,0:T(8,128)S(1)}, u32[]{:S(2)}, u32[]{:S(2)}) collective-permute-start(f32[4,64,64]{2,1,0:T(8,128)S(1)} %add_select_fusion.4), channel_id=1, source_target_pairs={{0,32},{16,48},{32,64},{48,80},{64,96},{80,112},{96,128},{112,144}... | collective-permute-start | bytes 196616 | tf_op jit(solution)/shard_map/ppermute | solution.py:20
  244.8 43.8 %copy-start.5 = (f32[2,64,4,64]{1,3,2,0:T(8,128)}, f32[2,64,4,64]{1,3,2,0:T(8,128)S(1)}, u32[]{:S(2)}) copy-start(f32[2,64,4,64]{1,3,2,0:T(8,128)S(1)} %copy.145) | copy-start | bytes 393220
  247.5 10.1 %collective-permute-start.9 = (f32[4,64,64]{2,1,0:T(8,128)S(1)}, f32[4,64,64]{2,1,0:T(8,128)S(1)}, u32[]{:S(2)}, u32[]{:S(2)}) collective-permute-start(f32[4,64,64]{2,1,0:T(8,128)S(1)} %add_select_fusion.3), channel_id=1, source_target_pairs={{0,64},{16,80},{32,96},{48,112},{64,128},{80,144},{96,160},{112,17... | collective-permute-start | bytes 196616 | tf_op jit(solution)/shard_map/ppermute | solution.py:20
  257.7 15.1 %collective-permute-start.10 = (f32[4,64,64]{2,1,0:T(8,128)S(1)}, f32[4,64,64]{2,1,0:T(8,128)S(1)}, u32[]{:S(2)}, u32[]{:S(2)}) collective-permute-start(f32[4,64,64]{2,1,0:T(8,128)S(1)} %add_select_fusion.2), channel_id=1, source_target_pairs={{0,128},{16,144},{32,160},{48,176},{64,192},{80,208},{96,224},{112... | collective-permute-start | bytes 196616 | tf_op jit(solution)/shard_map/ppermute | solution.py:20
  273.0 19.8 %copy-start.9 = (f32[4,64,64]{2,1,0:T(8,128)}, f32[4,64,64]{2,1,0:T(8,128)S(1)}, u32[]{:S(2)}) copy-start(f32[4,64,64]{2,1,0:T(8,128)S(1)} %add_select_fusion.1) | copy-start | bytes 196612
  273.0 26.8 %collective-permute-start.11 = (f32[4,64,64]{2,1,0:T(8,128)S(1)}, f32[4,64,64]{2,1,0:T(8,128)}, u32[]{:S(2)}, u32[]{:S(2)}) collective-permute-start(f32[4,64,64]{2,1,0:T(8,128)S(1)} %add_select_fusion.1), channel_id=1, source_target_pairs={{0,256},{16,272},{32,288},{48,304},{64,320},{80,336},{96,352},{112... | collective-permute-start | bytes 196616 | tf_op jit(solution)/shard_map/ppermute | solution.py:20
  289.5 8.7 %copy-start.1 = (bf16[1,16,2,128,256]{4,3,0,1,2:T(8,128)(2,1)S(1)}, bf16[1,16,2,128,256]{4,3,0,1,2:T(8,128)(2,1)}, u32[]{:S(2)}) copy-start(bf16[1,16,2,128,256]{4,3,0,1,2:T(8,128)(2,1)} %get-tuple-element.137) | copy-start | bytes 6291460
  298.2 1.6 copy-start.10
  298.2 1.6 copy-start.18
  298.2 1.6 copy-start.20
  298.2 3.4 copy-start.8
  299.7 7.7 %copy-start.4 = (bf16[257,4096]{1,0:T(8,128)(2,1)S(1)}, bf16[257,4096]{1,0:T(8,128)(2,1)}, u32[]{:S(2)}) copy-start(bf16[257,4096]{1,0:T(8,128)(2,1)} %all-gather.6.cloned.1.call-done) | copy-start | bytes 6316036
  299.7 7.7 %copy-start.30 = (f32[256]{0:T(256)S(1)}, f32[256]{0:T(256)}, u32[]{:S(2)}) copy-start(f32[256]{0:T(256)} %param.34) | copy-start | bytes 3076
  299.7 7.7 %copy-start.31 = (f32[256]{0:T(256)S(1)}, f32[256]{0:T(256)}, u32[]{:S(2)}) copy-start(f32[256]{0:T(256)} %param.33) | copy-start | bytes 3076
  299.7 7.7 %copy-start.32 = (pred[256]{0:T(512)(128)(4,1)S(1)}, pred[256]{0:T(512)(128)(4,1)}, u32[]{:S(2)}) copy-start(pred[256]{0:T(512)(128)(4,1)} %concatenate.22) | copy-start | bytes 772
  314.9 0.9 copy-start.6
  315.0 1.0 copy-start.17
  315.0 2.4 copy-start.11
  (2 other events, 1.4 us)
Sparse Core Ops, SparseCore 0:
  12.5 85.6 all-gather.7
  101.8 58.8 all-gather.5
  162.8 33.1 all-gather.9
  315.1 83.9 reduce-scatter.1
